TPU v7x, 512 devices: a whole 4x8x8 slice. The times are simulated.
512 devices in a mesh: dp: 16 (over z, core), mp: 32 (over y, x).
Axes of the slice: x: 4, y: 8, z: 8, core: 2. Of those that a mesh axis runs over, the one named last changes fastest.
Arguments:
- inputs: bfloat16 [32768, 4096], P('dp', 'mp'), may hold values from -6 to 6
- out_grad: bfloat16 [32768, 4096], P('dp', 'mp'), may hold values from -6 to 6
- mean_state: float32 [6, 64, 64, 64], P(None, 'mp', 'dp'), may hold values from -0.75 to 0.75
- hess_state: float32 [6, 64, 64, 64], P(None, 'mp', 'dp'), may hold values from 2 to 20
- grad_state: float32 [6, 64, 64, 64], P(None, 'mp', 'dp'), may hold values from -1.8 to 1.8
- noise_draw: float32 [16, 6, 64, 64, 64], P('dp', None, 'mp'), may hold values from -6 to 6
Outputs:
- new_mean: float32 [6, 64, 64, 64], P(None, 'mp', 'dp')
- new_hess: float32 [6, 64, 64, 64], P(None, 'mp', 'dp')
- new_grad: float32 [6, 64, 64, 64], P(None, 'mp', 'dp')
All inputs are finite; a program needn't handle non-finite values.
Results may differ from a plain program's by a relative error of at most 0.0018.
Values may be sent and summed in bfloat16 or wider, within the bound.
No kernel may reach another device: no remote copies, remote signals or barrier semaphores. Data moves between devices by JAX's collectives and lax.ppermute only.
A program may use at most 64 MiB of HBM per device.

v0:
```python
import jax
import jax.numpy as jnp
from jax import lax
from jax.sharding import PartitionSpec as P

LAMBDA_SIZE = 100.0
DELTA_DAMP = 0.001
BETA_GRAD = 0.9
BETA_HESS = 0.9
STEP_RATE = 1.0


def bdot(form, left, right):
    return jnp.einsum(form, left, right, preferred_element_type=jnp.float32)


def silu_slope(value):
    sigm = jax.nn.sigmoid(value)
    return sigm * (1.0 + value * (1.0 - sigm))


def per_device(inputs, out_grad, mean_state, hess_state, grad_state, noise_draw):
    tokens = inputs.shape[0]
    local_blocks = mean_state.shape[1]
    width = mean_state.shape[3]
    scale = tokens ** (-0.5)
    full_mean, full_hess = (
        lax.all_gather(mean_state, "dp", axis=2, tiled=True),
        lax.all_gather(hess_state, "dp", axis=2, tiled=True),
    )
    spread = jnp.sqrt(LAMBDA_SIZE * (full_hess + DELTA_DAMP))
    noise = noise_draw[0]
    sampled = (full_mean + noise / spread).astype(jnp.bfloat16)
    in_rows = inputs.reshape(tokens, local_blocks, width)
    grad_rows = out_grad.reshape(tokens, local_blocks, width)
    y_left = bdot("tbr,brc->tcb", in_rows, sampled[0]).astype(jnp.bfloat16)
    y_right = bdot("tbr,brc->tcb", in_rows, sampled[2]).astype(jnp.bfloat16)
    perm_left = lax.all_to_all(y_left, "mp", split_axis=1, concat_axis=2, tiled=True)
    perm_right = lax.all_to_all(y_right, "mp", split_axis=1, concat_axis=2, tiled=True)
    u_left = bdot("tji,jic->tjc", perm_left, sampled[1])
    u_right = bdot("tji,jic->tjc", perm_right, sampled[3])
    hidden = (jax.nn.silu(u_left) * u_right).astype(jnp.bfloat16)
    outer = bdot("tbr,brc->tcb", hidden, sampled[4]).astype(jnp.bfloat16)
    perm_left, perm_right, u_left, u_right, hidden, outer = (
        perm_left,
        perm_right,
        u_left,
        u_right,
        hidden,
        outer,
    )
    mixed_rows = lax.all_to_all(outer, "mp", split_axis=1, concat_axis=2, tiled=True)
    back_outer = bdot("tjc,jic->tij", grad_rows, sampled[5]).astype(jnp.bfloat16)
    back_hidden = lax.all_to_all(back_outer, "mp", split_axis=1, concat_axis=2, tiled=True)
    grad_five = bdot("tji,tjc->jic", mixed_rows, grad_rows) * scale
    grad_four = bdot("tbr,tbc->brc", hidden, back_hidden) * scale
    d_hidden = bdot("tbc,brc->tbr", back_hidden, sampled[4])
    gate_grad = (d_hidden * u_right * silu_slope(u_left)).astype(jnp.bfloat16)
    value_grad = (d_hidden * jax.nn.silu(u_left)).astype(jnp.bfloat16)
    grad_one = bdot("tji,tjc->jic", perm_left, gate_grad) * scale
    grad_three = bdot("tji,tjc->jic", perm_right, value_grad) * scale
    back_left = bdot("tjc,jic->tij", gate_grad, sampled[1]).astype(jnp.bfloat16)
    back_right = bdot("tjc,jic->tij", value_grad, sampled[3]).astype(jnp.bfloat16)
    rows_left, rows_right = (
        lax.all_to_all(back_left, "mp", split_axis=1, concat_axis=2, tiled=True),
        lax.all_to_all(back_right, "mp", split_axis=1, concat_axis=2, tiled=True),
    )
    grad_zero = bdot("tbr,tbc->brc", in_rows, rows_left) * scale
    grad_two = bdot("tbr,tbc->brc", in_rows, rows_right) * scale
    all_grads = jnp.stack([grad_zero, grad_one, grad_two, grad_three, grad_four, grad_five])
    grad_sum, hess_sum = (
        lax.psum_scatter(all_grads, "dp", scatter_dimension=2, tiled=True),
        lax.psum_scatter(all_grads * noise * spread, "dp", scatter_dimension=2, tiled=True),
    )
    groups = lax.axis_size("dp")
    grad_avg = grad_sum / groups
    hess_avg = hess_sum / groups
    new_grad = BETA_GRAD * grad_state + (1.0 - BETA_GRAD) * grad_avg
    new_hess = (
        BETA_HESS * hess_state
        + (1.0 - BETA_HESS) * hess_avg
        + 0.5 * (1.0 - BETA_HESS) ** 2 * (hess_state - hess_avg) ** 2 / (hess_state + DELTA_DAMP)
    )
    new_mean = mean_state - STEP_RATE * (new_grad + DELTA_DAMP * mean_state) / (
        new_hess + DELTA_DAMP
    )
    return (new_mean, new_hess, new_grad)


def solution(mesh):
    return jax.shard_map(
        per_device,
        mesh=mesh,
        in_specs=(
            P("dp", "mp"),
            P("dp", "mp"),
            P(None, "mp", "dp", None),
            P(None, "mp", "dp", None),
            P(None, "mp", "dp", None),
            P("dp", None, "mp", None, None),
        ),
        out_specs=(P(None, "mp", "dp", None), P(None, "mp", "dp", None), P(None, "mp", "dp", None)),
        check_vma=False,
    )
```

profile of v0, /device:TPU:1, one launch (start us, length us, event | category | flops | bytes accessed | tf_op | source)
XLA Modules:
  0.0 319.1 jit_solution(12250809010809188880)
XLA Ops:
  8.0 25.6 %all_gather.7 = f32[6,2,64,64]{3,1,0,2:T(2,128)S(1)} all-gather(f32[6,2,4,64]{3,1,0,2:T(2,128)S(1)} %copy.44), channel_id=1, replica_groups=mesh['dp'=16,'mp'=32] {'dp'}, dimensions={2}, use_global_device_ids=true | all-gather | bytes 208896 | tf_op jit(solution)/shard_map/all_gather | solution.py:29
  34.3 15.5 %all_gather.6 = f32[6,2,64,64]{3,1,0,2:T(2,128)S(1)} all-gather(f32[6,2,4,64]{3,1,0,2:T(2,128)S(1)} %copy.43), channel_id=1, replica_groups=mesh['dp'=16,'mp'=32] {'dp'}, dimensions={2}, use_global_device_ids=true | all-gather | bytes 208896 | tf_op jit(solution)/shard_map/all_gather | solution.py:28
  51.4 1.4 copy.56
  52.7 9.8 %all-to-all-start.2 = ((bf16[2048,64,2]{0,2,1:T(2,128)(2,1)}), bf16[2048,64,2]{0,2,1:T(2,128)(2,1)S(1)}, u32[]{:S(2)}, u32[]{:S(2)}) async-start(bf16[2048,64,2]{0,2,1:T(2,128)(2,1)} %copy.56), calls=%async_computation.2 | async-start | bytes 1048576 | tf_op jit(solution)/shard_map/all_to_all | solution.py:38
  63.1 1.4 copy.48
  64.4 14.8 %all-to-all-done.2 = bf16[2048,64,2]{0,2,1:T(2,128)(2,1)S(1)} async-done(((bf16[2048,64,2]{0,2,1:T(2,128)(2,1)}), bf16[2048,64,2]{0,2,1:T(2,128)(2,1)S(1)}, u32[]{:S(2)}, u32[]{:S(2)}) %all-to-all-start.2) | async-done | bytes 524320 | tf_op jit(solution)/shard_map/all_to_all | solution.py:38
  79.2 5.1 %all-to-all-start = ((bf16[2048,64,2]{0,2,1:T(2,128)(2,1)}), bf16[2048,64,2]{0,2,1:T(2,128)(2,1)S(1)}, u32[]{:S(2)}, u32[]{:S(2)}) async-start(bf16[2048,64,2]{0,2,1:T(2,128)(2,1)} %copy.48), calls=%async_computation | async-start | bytes 1048576 | tf_op jit(solution)/shard_map/all_to_all | solution.py:54
  86.0 13.7 %all-to-all-done = bf16[2048,64,2]{0,2,1:T(2,128)(2,1)S(1)} async-done(((bf16[2048,64,2]{0,2,1:T(2,128)(2,1)}), bf16[2048,64,2]{0,2,1:T(2,128)(2,1)S(1)}, u32[]{:S(2)}, u32[]{:S(2)}) %all-to-all-start) | async-done | bytes 524320 | tf_op jit(solution)/shard_map/all_to_all | solution.py:54
  99.8 6.1 %all-to-all-start.1 = ((bf16[2048,64,2]{0,2,1:T(2,128)(2,1)}), bf16[2048,64,2]{0,2,1:T(2,128)(2,1)S(1)}, u32[]{:S(2)}, u32[]{:S(2)}) async-start(bf16[2048,64,2]{0,2,1:T(2,128)(2,1)} %copy.52), calls=%async_computation.1 | async-start | bytes 1048576 | tf_op jit(solution)/shard_map/all_to_all | solution.py:39
  107.0 2.1 convolution_bitcast_fusion
  109.1 2.0 convolution_bitcast_fusion.2
  111.1 10.0 %all-to-all-done.1 = bf16[2048,64,2]{0,2,1:T(2,128)(2,1)S(1)} async-done(((bf16[2048,64,2]{0,2,1:T(2,128)(2,1)}), bf16[2048,64,2]{0,2,1:T(2,128)(2,1)S(1)}, u32[]{:S(2)}, u32[]{:S(2)}) %all-to-all-start.1) | async-done | bytes 524320 | tf_op jit(solution)/shard_map/all_to_all | solution.py:39
  121.7 3.1 multiply_convert_fusion
  125.8 1.4 copy.59
  127.1 6.4 %all-to-all-start.3 = ((bf16[2048,64,2]{0,2,1:T(2,128)(2,1)}), bf16[2048,64,2]{0,2,1:T(2,128)(2,1)}, u32[]{:S(2)}, u32[]{:S(2)}) async-start(bf16[2048,64,2]{0,2,1:T(2,128)(2,1)} %copy.59), calls=%async_computation.3 | async-start | bytes 1048576 | tf_op jit(solution)/shard_map/all_to_all | solution.py:65
  136.2 12.5 %all-to-all-done.3 = bf16[2048,64,2]{0,2,1:T(2,128)(2,1)} async-done(((bf16[2048,64,2]{0,2,1:T(2,128)(2,1)}), bf16[2048,64,2]{0,2,1:T(2,128)(2,1)}, u32[]{:S(2)}, u32[]{:S(2)}) %all-to-all-start.3) | async-done | bytes 524320 | tf_op jit(solution)/shard_map/all_to_all | solution.py:65
  148.7 6.6 %all-to-all-start.4 = ((bf16[2048,64,2]{0,2,1:T(2,128)(2,1)}), bf16[2048,64,2]{0,2,1:T(2,128)(2,1)}, u32[]{:S(2)}, u32[]{:S(2)}) async-start(bf16[2048,64,2]{0,2,1:T(2,128)(2,1)} %copy.61), calls=%async_computation.4 | async-start | bytes 1048576 | tf_op jit(solution)/shard_map/all_to_all | solution.py:66
  156.5 1.4 copy.64
  157.8 2.2 copy.95
  160.0 2.0 all_to_all.93
  162.1 1.9 fusion.15
  164.0 6.4 %all-to-all-done.4 = bf16[2048,64,2]{0,2,1:T(2,128)(2,1)} async-done(((bf16[2048,64,2]{0,2,1:T(2,128)(2,1)}), bf16[2048,64,2]{0,2,1:T(2,128)(2,1)}, u32[]{:S(2)}, u32[]{:S(2)}) %all-to-all-start.4) | async-done | bytes 524320 | tf_op jit(solution)/shard_map/all_to_all | solution.py:66
  170.4 6.3 %all-to-all-start.5 = ((bf16[2048,64,2]{0,2,1:T(2,128)(2,1)}), bf16[2048,64,2]{0,2,1:T(2,128)(2,1)}, u32[]{:S(2)}, u32[]{:S(2)}) async-start(bf16[2048,64,2]{0,2,1:T(2,128)(2,1)} %copy.64), calls=%async_computation.5 | async-start | bytes 1048576 | tf_op jit(solution)/shard_map/all_to_all | solution.py:52
  176.7 2.2 copy.94
  178.9 2.0 all_to_all.97
  180.9 2.0 fusion.12
  185.2 2.0 fusion.14
  189.7 2.0 all-to-all-done.5
  191.7 1.4 copy.93
  194.3 1.9 fusion.19
  198.2 112.6 %all-reduce.5.cloned.1.call-done = (f32[6,2,64,64]{3,2,1,0:T(8,128)}, f32[6,2,64,64]{3,2,1,0:T(8,128)}) async-done(((f32[6,2,64,64]{3,2,1,0:T(8,128)}, f32[6,2,64,64]{3,2,1,0:T(8,128)}), (f32[6,2,64,64]{3,2,1,0:T(8,128)}, f32[6,2,64,64]{3,2,1,0:T(8,128)})) %all-reduce.5.cloned.1.call-update) | async-done | bytes 393232
  310.7 1.5 divide_subtract_fusion
  (54 shorter events, 19.0 us)
Async XLA Ops:
  7.2 42.7 %copy-start.5 = (bf16[2048,128]{1,0:T(8,128)(2,1)S(1)}, bf16[2048,128]{1,0:T(8,128)(2,1)}, u32[]{:S(2)}) copy-start(bf16[2048,128]{1,0:T(8,128)(2,1)} %param.6) | copy-start | bytes 1572868
  49.8 1.0 copy-start.2
  51.0 33.3 %copy-start.4 = (bf16[6,2,64,64]{3,2,1,0:T(8,128)(2,1)}, bf16[6,2,64,64]{3,2,1,0:T(8,128)(2,1)S(1)}, u32[]{:S(2)}) copy-start(bf16[6,2,64,64]{3,2,1,0:T(8,128)(2,1)S(1)} %fusion.18) | copy-start | bytes 294916
  52.7 9.8 %copy-start.6 = (bf16[2048,128]{1,0:T(8,128)(2,1)S(1)}, bf16[2048,128]{1,0:T(8,128)(2,1)}, u32[]{:S(2)}) copy-start(bf16[2048,128]{1,0:T(8,128)(2,1)} %param.7) | copy-start | bytes 1572868
  52.7 26.5 %all-to-all-start.2 = ((bf16[2048,64,2]{0,2,1:T(2,128)(2,1)}), bf16[2048,64,2]{0,2,1:T(2,128)(2,1)S(1)}, u32[]{:S(2)}, u32[]{:S(2)}) async-start(bf16[2048,64,2]{0,2,1:T(2,128)(2,1)} %copy.56), calls=%async_computation.2 | async-start | bytes 1048576 | tf_op jit(solution)/shard_map/all_to_all | solution.py:38
  79.2 20.5 %all-to-all-start = ((bf16[2048,64,2]{0,2,1:T(2,128)(2,1)}), bf16[2048,64,2]{0,2,1:T(2,128)(2,1)S(1)}, u32[]{:S(2)}, u32[]{:S(2)}) async-start(bf16[2048,64,2]{0,2,1:T(2,128)(2,1)} %copy.48), calls=%async_computation | async-start | bytes 1048576 | tf_op jit(solution)/shard_map/all_to_all | solution.py:54
  99.8 21.3 %all-to-all-start.1 = ((bf16[2048,64,2]{0,2,1:T(2,128)(2,1)}), bf16[2048,64,2]{0,2,1:T(2,128)(2,1)S(1)}, u32[]{:S(2)}, u32[]{:S(2)}) async-start(bf16[2048,64,2]{0,2,1:T(2,128)(2,1)} %copy.52), calls=%async_computation.1 | async-start | bytes 1048576 | tf_op jit(solution)/shard_map/all_to_all | solution.py:39
  124.7 1.0 copy-start.1
  127.1 21.6 %all-to-all-start.3 = ((bf16[2048,64,2]{0,2,1:T(2,128)(2,1)}), bf16[2048,64,2]{0,2,1:T(2,128)(2,1)}, u32[]{:S(2)}, u32[]{:S(2)}) async-start(bf16[2048,64,2]{0,2,1:T(2,128)(2,1)} %copy.59), calls=%async_computation.3 | async-start | bytes 1048576 | tf_op jit(solution)/shard_map/all_to_all | solution.py:65
  148.7 21.6 %all-to-all-start.4 = ((bf16[2048,64,2]{0,2,1:T(2,128)(2,1)}), bf16[2048,64,2]{0,2,1:T(2,128)(2,1)}, u32[]{:S(2)}, u32[]{:S(2)}) async-start(bf16[2048,64,2]{0,2,1:T(2,128)(2,1)} %copy.61), calls=%async_computation.4 | async-start | bytes 1048576 | tf_op jit(solution)/shard_map/all_to_all | solution.py:66
  170.4 21.3 %all-to-all-start.5 = ((bf16[2048,64,2]{0,2,1:T(2,128)(2,1)}), bf16[2048,64,2]{0,2,1:T(2,128)(2,1)}, u32[]{:S(2)}, u32[]{:S(2)}) async-start(bf16[2048,64,2]{0,2,1:T(2,128)(2,1)} %copy.64), calls=%async_computation.5 | async-start | bytes 1048576 | tf_op jit(solution)/shard_map/all_to_all | solution.py:52
  176.6 134.1 %all-reduce.5.cloned.1.call-start = ((), (), s32[]{:S(2)}) async-start(), calls=%async_computation.6 | async-start | bytes 1572864
  182.9 1.0 copy-start.7
  185.2 2.0 copy-start.8
  185.2 2.7 copy-start
  193.3 1.0 copy-start.3
  196.2 114.5 %copy-start.10 = (f32[6,2,4,64]{3,2,1,0:T(4,128)S(1)}, f32[6,2,4,64]{3,2,1,0:T(4,128)}, u32[]{:S(2)}) copy-start(f32[6,2,4,64]{3,2,1,0:T(4,128)} %param.9) | copy-start | bytes 36868
  196.2 114.5 %copy-start.11 = (f32[6,2,4,64]{3,2,1,0:T(4,128)S(1)}, f32[6,2,4,64]{3,2,1,0:T(4,128)}, u32[]{:S(2)}) copy-start(f32[6,2,4,64]{3,2,1,0:T(4,128)} %param.10) | copy-start | bytes 36868
  196.2 114.5 %copy-start.9 = (f32[6,2,4,64]{3,2,1,0:T(4,128)S(1)}, f32[6,2,4,64]{3,2,1,0:T(4,128)}, u32[]{:S(2)}) copy-start(f32[6,2,4,64]{3,2,1,0:T(4,128)} %param.8) | copy-start | bytes 36868
Sparse Core Ops, SparseCore 0:
  196.3 114.3 all-reduce.4
where the time goes:
time: 321 us; the launch traced here: 319 us
  waiting for transfers between devices  172 us (54%)
  blocking collectives  41.1 us (13%)
  starting transfers between devices  40.3 us (13%)
  local copies, waits for them, and re-layouts  27 us (8%)
  matrix products  20.2 us (6%)
  between operations  14.9 us (5%)
  other arithmetic  3.57 us (1%)
    unnamed x2, waiting for transfers between devices  113 us
    all_gather x1, blocking collectives, per_device(): lax.all_gather(hess_state, 'dp', axis=2, tiled=True)  25.6 us
    dot_general x15, matrix products, bdot(): return jnp.einsum(form, left, right, preferred_element_type=jnp.float32)  20.2 us
    all_gather x1, blocking collectives, per_device(): lax.all_gather(mean_state, 'dp', axis=2, tiled=True)  15.5 us
    all_to_all x1, waiting for transfers between devices, per_device(): lax.all_to_all(y_left, 'mp', split_axis=1, concat_axis=2, tiled=True)  14.8 us
    all_to_all x1, waiting for transfers between devices, per_device(): lax.all_to_all(back_outer, 'mp', split_axis=1, concat_axis=2, tiled=True)  13.7 us
    all_to_all x1, waiting for transfers between devices, per_device(): lax.all_to_all(back_left, 'mp', split_axis=1, concat_axis=2, tiled=True)  12.5 us
    all_to_all x1, waiting for transfers between devices, per_device(): lax.all_to_all(y_right, 'mp', split_axis=1, concat_axis=2, tiled=True)  9.96 us
  transfers between devices with their start and end apart: 7, of which 7 were waited for; matrix products, arithmetic and copies ran while one was open for 9% of the time, Pallas kernels for 0%

commit v1 on v0

--- a/solution.py
+++ b/solution.py
@@ -1,3 +1,4 @@
+import functools
 import jax
 import jax.numpy as jnp
 from jax import lax
@@ -8,6 +9,47 @@
 BETA_GRAD = 0.9
 BETA_HESS = 0.9
 STEP_RATE = 1.0
+
+
+def link_table(content, chip_axis, out_dim):
+    piece_next, carry, p_next = (
+        lax.axis_size(chip_axis),
+        lax.axis_index(chip_axis),
+        content.shape[out_dim],
+    )
+    value_now = lax.dynamic_update_slice_in_dim(
+        jnp.zeros(
+            [
+                hop_no * piece_next if nth == out_dim else hop_no
+                for nth, hop_no in enumerate(content.shape)
+            ],
+            content.dtype,
+        ),
+        content,
+        carry * p_next,
+        axis=out_dim,
+    )
+    local_out = before = content
+    s = 1
+    while s < piece_next // 2 + 1:
+        local_out = lax.ppermute(
+            local_out, chip_axis, perm=[(nth, (nth + 1) % piece_next) for nth in range(piece_next)]
+        )
+        value_now = lax.dynamic_update_slice_in_dim(
+            value_now, local_out, (carry - s) % piece_next * p_next, axis=out_dim
+        )
+        if 2 * s < piece_next:
+            before = lax.ppermute(
+                before, chip_axis, [(nth, (nth - 1) % piece_next) for nth in range(piece_next)]
+            )
+            value_now = lax.dynamic_update_slice_in_dim(
+                value_now, before, (carry + s) % piece_next * p_next, axis=out_dim
+            )
+        s += 1
+    return value_now
+
+
+notes_enter = functools.partial(link_table, chip_axis="dp", out_dim=2)
 
 
 def bdot(form, left, right):
@@ -26,7 +68,7 @@
     scale = tokens ** (-0.5)
     full_mean, full_hess = (
         lax.all_gather(mean_state, "dp", axis=2, tiled=True),
-        lax.all_gather(hess_state, "dp", axis=2, tiled=True),
+        notes_enter(hess_state),
     )
     spread = jnp.sqrt(LAMBDA_SIZE * (full_hess + DELTA_DAMP))
     noise = noise_draw[0]

time: 321 us -> 340 us (1.059)
  starting transfers between devices: 40.3 us -> 61.9 us
  blocking collectives: 41.1 us -> 20.4 us
  waiting for transfers between devices: 172 us -> 191 us
    all_gather x1 -> x0, blocking collectives: 25.6 us -> none  [per_device(): lax.all_gather(hess_state, 'dp', axis=2, tiled=True)]
    ppermute x0 -> x15, starting transfers between devices: none -> 25.4 us  [the longest x7 18.6 us: link_table(): lax.ppermute(before, chip_axis, [(nth, (nth - 1) % piece_next) for nth in...]
    unnamed x2, waiting for transfers between devices: 113 us -> 132 us
    all_to_all x1, waiting for transfers between devices: 12.5 us -> 0.92 us  [per_device(): lax.all_to_all(back_left, 'mp', split_axis=1, concat_axis=2, tiled=True)]
    ppermute x0 -> x15, waiting for transfers between devices: none -> 8.91 us  [the longest x8 8.15 us: link_table(): lax.ppermute(local_out, chip_axis, perm=[(nth, (nth + 1) % piece_next) fo...]
    all_to_all x1, waiting for transfers between devices: 1.99 us -> 10.1 us  [per_device(): lax.all_to_all(outer, 'mp', split_axis=1, concat_axis=2, tiled=True)]
    all_gather x1, blocking collectives: 15.5 us -> 20.4 us  [per_device(): lax.all_gather(mean_state, 'dp', axis=2, tiled=True)]
    all_to_all x1, starting transfers between devices: 5.07 us -> 9.8 us  [per_device(): lax.all_to_all(back_outer, 'mp', split_axis=1, concat_axis=2, tiled=True)]
  transfers between devices with their start and end apart: 7 -> 22, of which waited for: 7 -> 18; matrix products, arithmetic and copies ran while one was open for 9% -> 7% of each run, Pallas kernels for 0% -> 0%
where the time goes in v1:
time: 340 us; the launch traced here: 339 us
  waiting for transfers between devices  191 us (56%)
  starting transfers between devices  61.9 us (18%)
  local copies, waits for them, and re-layouts  29.2 us (9%)
  blocking collectives  20.4 us (6%)
  matrix products  18.2 us (5%)
  between operations  15.4 us (5%)
    unnamed x2, waiting for transfers between devices  132 us
    all_gather x1, blocking collectives, per_device(): lax.all_gather(mean_state, 'dp', axis=2, tiled=True)  20.4 us
    ppermute x7, starting transfers between devices, link_table(): lax.ppermute(before, chip_axis, [(nth, (nth - 1) % piece_next) for nth in...  18.6 us
    dot_general x15, matrix products, bdot(): return jnp.einsum(form, left, right, preferred_element_type=jnp.float32)  18.2 us
    all_to_all x1, waiting for transfers between devices, per_device(): lax.all_to_all(y_left, 'mp', split_axis=1, concat_axis=2, tiled=True)  11.1 us
    all_to_all x1, waiting for transfers between devices, per_device(): lax.all_to_all(back_outer, 'mp', split_axis=1, concat_axis=2, tiled=True)  10.8 us
    all_to_all x1, waiting for transfers between devices, per_device(): lax.all_to_all(outer, 'mp', split_axis=1, concat_axis=2, tiled=True)  10.1 us
    all_to_all x1, waiting for transfers between devices, per_device(): lax.all_to_all(back_right, 'mp', split_axis=1, concat_axis=2, tiled=True)  10 us
  transfers between devices with their start and end apart: 22, of which 18 were waited for; matrix products, arithmetic and copies ran while one was open for 7% of the time, Pallas kernels for 0%

profile of v1, /device:TPU:1, one launch (start us, length us, event | category | flops | bytes accessed | tf_op | source)
XLA Modules:
  0.0 338.8 jit_solution(17640364748662667432)
XLA Ops:
  7.2 3.5 %collective-permute-start = (f32[6,2,4,64]{3,2,1,0:T(4,128)}, f32[6,2,4,64]{3,2,1,0:T(4,128)S(1)}, u32[]{:S(2)}, u32[]{:S(2)}) collective-permute-start(f32[6,2,4,64]{3,2,1,0:T(4,128)} %param.9), channel_id=1, source_target_pairs={{0,32},{32,64},{64,96},{96,128},{128,160},{160,192},{192,224},{224... | collective-permute-start | bytes 36872 | tf_op jit(solution)/shard_map/ppermute | solution.py:35
  10.7 3.4 %collective-permute-start.1 = (f32[6,2,4,64]{3,2,1,0:T(4,128)}, f32[6,2,4,64]{3,2,1,0:T(4,128)S(1)}, u32[]{:S(2)}, u32[]{:S(2)}) collective-permute-start(f32[6,2,4,64]{3,2,1,0:T(4,128)} %param.9), channel_id=1, source_target_pairs={{0,480},{32,0},{64,32},{96,64},{128,96},{160,128},{192,160},{224,1... | collective-permute-start | bytes 36872 | tf_op jit(solution)/shard_map/ppermute | solution.py:42
  14.1 20.4 %all_gather.3 = f32[6,2,64,64]{3,1,0,2:T(2,128)S(1)} all-gather(f32[6,2,4,64]{3,1,0,2:T(2,128)S(1)} %copy.43), channel_id=1, replica_groups=mesh['dp'=16,'mp'=32] {'dp'}, dimensions={2}, use_global_device_ids=true | all-gather | bytes 208896 | tf_op jit(solution)/shard_map/all_gather | solution.py:70
  37.1 2.1 collective-permute-start.4
  42.5 2.6 collective-permute-start.7
  45.9 3.6 %collective-permute-start.9 = (f32[6,2,4,64]{3,2,1,0:T(4,128)S(1)}, f32[6,2,4,64]{3,2,1,0:T(4,128)S(1)}, u32[]{:S(2)}, u32[]{:S(2)}) collective-permute-start(f32[6,2,4,64]{3,2,1,0:T(4,128)S(1)} %collective-permute-done.7), channel_id=1, source_target_pairs={{0,480},{32,0},{64,32},{96,64},{128,96},{160,128},{192,160},{224,1... | collective-permute-start | bytes 36872 | tf_op jit(solution)/shard_map/ppermute | solution.py:42
  50.3 3.6 %collective-permute-start.11 = (f32[6,2,4,64]{3,2,1,0:T(4,128)S(1)}, f32[6,2,4,64]{3,2,1,0:T(4,128)S(1)}, u32[]{:S(2)}, u32[]{:S(2)}) collective-permute-start(f32[6,2,4,64]{3,2,1,0:T(4,128)S(1)} %collective-permute-done.9), channel_id=1, source_target_pairs={{0,480},{32,0},{64,32},{96,64},{128,96},{160,128},{192,160},{224,1... | collective-permute-start | bytes 36872 | tf_op jit(solution)/shard_map/ppermute | solution.py:42
  54.8 3.6 %collective-permute-start.13 = (f32[6,2,4,64]{3,2,1,0:T(4,128)S(1)}, f32[6,2,4,64]{3,2,1,0:T(4,128)S(1)}, u32[]{:S(2)}, u32[]{:S(2)}) collective-permute-start(f32[6,2,4,64]{3,2,1,0:T(4,128)S(1)} %collective-permute-done.11), channel_id=1, source_target_pairs={{0,480},{32,0},{64,32},{96,64},{128,96},{160,128},{192,160},{224,1... | collective-permute-start | bytes 36872 | tf_op jit(solution)/shard_map/ppermute | solution.py:42
  59.3 4.3 %collective-permute-done.14 = f32[6,2,4,64]{3,2,1,0:T(4,128)S(1)} collective-permute-done((f32[6,2,4,64]{3,2,1,0:T(4,128)S(1)}, f32[6,2,4,64]{3,2,1,0:T(4,128)S(1)}, u32[]{:S(2)}, u32[]{:S(2)}) %collective-permute-start.14) | collective-permute-done | bytes 12320 | tf_op jit(solution)/shard_map/ppermute | solution.py:35
  65.4 9.8 %all-to-all-start = ((bf16[2048,64,2]{0,2,1:T(2,128)(2,1)}), bf16[2048,64,2]{0,2,1:T(2,128)(2,1)S(1)}, u32[]{:S(2)}, u32[]{:S(2)}) async-start(bf16[2048,64,2]{0,2,1:T(2,128)(2,1)} %copy.46), calls=%async_computation | async-start | bytes 1048576 | tf_op jit(solution)/shard_map/all_to_all | solution.py:96
  77.1 10.8 %all-to-all-done = bf16[2048,64,2]{0,2,1:T(2,128)(2,1)S(1)} async-done(((bf16[2048,64,2]{0,2,1:T(2,128)(2,1)}), bf16[2048,64,2]{0,2,1:T(2,128)(2,1)S(1)}, u32[]{:S(2)}, u32[]{:S(2)}) %all-to-all-start) | async-done | bytes 524320 | tf_op jit(solution)/shard_map/all_to_all | solution.py:96
  88.0 6.1 %all-to-all-start.2 = ((bf16[2048,64,2]{0,2,1:T(2,128)(2,1)}), bf16[2048,64,2]{0,2,1:T(2,128)(2,1)S(1)}, u32[]{:S(2)}, u32[]{:S(2)}) async-start(bf16[2048,64,2]{0,2,1:T(2,128)(2,1)} %copy.54), calls=%async_computation.2 | async-start | bytes 1048576 | tf_op jit(solution)/shard_map/all_to_all | solution.py:80
  95.8 11.1 %all-to-all-done.2 = bf16[2048,64,2]{0,2,1:T(2,128)(2,1)S(1)} async-done(((bf16[2048,64,2]{0,2,1:T(2,128)(2,1)}), bf16[2048,64,2]{0,2,1:T(2,128)(2,1)S(1)}, u32[]{:S(2)}, u32[]{:S(2)}) %all-to-all-start.2) | async-done | bytes 524320 | tf_op jit(solution)/shard_map/all_to_all | solution.py:80
  106.9 5.9 %all-to-all-start.1 = ((bf16[2048,64,2]{0,2,1:T(2,128)(2,1)}), bf16[2048,64,2]{0,2,1:T(2,128)(2,1)S(1)}, u32[]{:S(2)}, u32[]{:S(2)}) async-start(bf16[2048,64,2]{0,2,1:T(2,128)(2,1)} %copy.50), calls=%async_computation.1 | async-start | bytes 1048576 | tf_op jit(solution)/shard_map/all_to_all | solution.py:81
  113.9 2.0 convolution_bitcast_fusion.2
  116.0 2.1 convolution_bitcast_fusion
  118.1 7.6 %all-to-all-done.1 = bf16[2048,64,2]{0,2,1:T(2,128)(2,1)S(1)} async-done(((bf16[2048,64,2]{0,2,1:T(2,128)(2,1)}), bf16[2048,64,2]{0,2,1:T(2,128)(2,1)S(1)}, u32[]{:S(2)}, u32[]{:S(2)}) %all-to-all-start.1) | async-done | bytes 524320 | tf_op jit(solution)/shard_map/all_to_all | solution.py:81
  126.2 3.2 multiply_convert_fusion
  131.9 5.2 %all-to-all-start.5 = ((bf16[2048,64,2]{0,2,1:T(2,128)(2,1)}), bf16[2048,64,2]{0,2,1:T(2,128)(2,1)}, u32[]{:S(2)}, u32[]{:S(2)}) async-start(bf16[2048,64,2]{0,2,1:T(2,128)(2,1)} %copy.62), calls=%async_computation.5 | async-start | bytes 1048576 | tf_op jit(solution)/shard_map/all_to_all | solution.py:94
  139.8 10.1 %all-to-all-done.5 = bf16[2048,64,2]{0,2,1:T(2,128)(2,1)} async-done(((bf16[2048,64,2]{0,2,1:T(2,128)(2,1)}), bf16[2048,64,2]{0,2,1:T(2,128)(2,1)}, u32[]{:S(2)}, u32[]{:S(2)}) %all-to-all-start.5) | async-done | bytes 524320 | tf_op jit(solution)/shard_map/all_to_all | solution.py:94
  149.9 4.8 %all-to-all-start.4 = ((bf16[2048,64,2]{0,2,1:T(2,128)(2,1)}), bf16[2048,64,2]{0,2,1:T(2,128)(2,1)}, u32[]{:S(2)}, u32[]{:S(2)}) async-start(bf16[2048,64,2]{0,2,1:T(2,128)(2,1)} %copy.59), calls=%async_computation.4 | async-start | bytes 1048576 | tf_op jit(solution)/shard_map/all_to_all | solution.py:108
  157.4 10.0 %all-to-all-done.4 = bf16[2048,64,2]{0,2,1:T(2,128)(2,1)} async-done(((bf16[2048,64,2]{0,2,1:T(2,128)(2,1)}), bf16[2048,64,2]{0,2,1:T(2,128)(2,1)}, u32[]{:S(2)}, u32[]{:S(2)}) %all-to-all-start.4) | async-done | bytes 524320 | tf_op jit(solution)/shard_map/all_to_all | solution.py:108
  167.4 4.6 %all-to-all-start.3 = ((bf16[2048,64,2]{0,2,1:T(2,128)(2,1)}), bf16[2048,64,2]{0,2,1:T(2,128)(2,1)}, u32[]{:S(2)}, u32[]{:S(2)}) async-start(bf16[2048,64,2]{0,2,1:T(2,128)(2,1)} %copy.57), calls=%async_computation.3 | async-start | bytes 1048576 | tf_op jit(solution)/shard_map/all_to_all | solution.py:107
  172.1 2.2 copy.82
  174.3 2.0 all_to_all.101
  176.3 2.2 copy.83
  178.5 2.0 all_to_all.97
  180.5 2.0 fusion.12
  185.0 2.2 copy.84
  187.2 2.1 all_to_all.93
  189.2 2.0 fusion.15
  198.8 131.6 %all-reduce.5.cloned.1.call-done = (f32[6,2,64,64]{3,2,1,0:T(8,128)}, f32[6,2,64,64]{3,2,1,0:T(8,128)}) async-done(((f32[6,2,64,64]{3,2,1,0:T(8,128)}, f32[6,2,64,64]{3,2,1,0:T(8,128)}), (f32[6,2,64,64]{3,2,1,0:T(8,128)}, f32[6,2,64,64]{3,2,1,0:T(8,128)})) %all-reduce.5.cloned.1.call-update) | async-done | bytes 393232
  (103 shorter events, 34.7 us)
Async XLA Ops:
  7.2 6.9 %copy-start.9 = (f32[6,2,4,64]{3,2,1,0:T(4,128)S(1)}, f32[6,2,4,64]{3,2,1,0:T(4,128)}, u32[]{:S(2)}) copy-start(f32[6,2,4,64]{3,2,1,0:T(4,128)} %param.8) | copy-start | bytes 36868
  7.2 28.7 %collective-permute-start = (f32[6,2,4,64]{3,2,1,0:T(4,128)}, f32[6,2,4,64]{3,2,1,0:T(4,128)S(1)}, u32[]{:S(2)}, u32[]{:S(2)}) collective-permute-start(f32[6,2,4,64]{3,2,1,0:T(4,128)} %param.9), channel_id=1, source_target_pairs={{0,32},{32,64},{64,96},{96,128},{128,160},{160,192},{192,224},{224... | collective-permute-start | bytes 36872 | tf_op jit(solution)/shard_map/ppermute | solution.py:35
  10.7 25.3 %collective-permute-start.1 = (f32[6,2,4,64]{3,2,1,0:T(4,128)}, f32[6,2,4,64]{3,2,1,0:T(4,128)S(1)}, u32[]{:S(2)}, u32[]{:S(2)}) collective-permute-start(f32[6,2,4,64]{3,2,1,0:T(4,128)} %param.9), channel_id=1, source_target_pairs={{0,480},{32,0},{64,32},{96,64},{128,96},{160,128},{192,160},{224,1... | collective-permute-start | bytes 36872 | tf_op jit(solution)/shard_map/ppermute | solution.py:42
  14.1 20.5 %copy-start.11 = (f32[6,2,4,64]{3,2,1,0:T(4,128)S(1)}, f32[6,2,4,64]{3,2,1,0:T(4,128)}, u32[]{:S(2)}) copy-start(f32[6,2,4,64]{3,2,1,0:T(4,128)} %param.9) | copy-start | bytes 36868
  35.8 27.8 %copy-start.3 = (f32[1,6,2,64,64]{4,3,2,1,0:T(8,128)S(1)}, f32[1,6,2,64,64]{4,3,2,1,0:T(8,128)}, u32[]{:S(2)}) copy-start(f32[1,6,2,64,64]{4,3,2,1,0:T(8,128)} %param.11) | copy-start | bytes 589828
  35.9 1.2 collective-permute-start.2
  35.9 3.3 collective-permute-start.3
  37.1 4.1 %collective-permute-start.4 = (f32[6,2,4,64]{3,2,1,0:T(4,128)S(1)}, f32[6,2,4,64]{3,2,1,0:T(4,128)S(1)}, u32[]{:S(2)}, u32[]{:S(2)}) collective-permute-start(f32[6,2,4,64]{3,2,1,0:T(4,128)S(1)} %collective-permute-done.2), channel_id=1, source_target_pairs={{0,32},{32,64},{64,96},{96,128},{128,160},{160,192},{192,224},{224... | collective-permute-start | bytes 36872 | tf_op jit(solution)/shard_map/ppermute | solution.py:35
  39.2 3.3 collective-permute-start.5
  41.2 4.5 %collective-permute-start.6 = (f32[6,2,4,64]{3,2,1,0:T(4,128)S(1)}, f32[6,2,4,64]{3,2,1,0:T(4,128)S(1)}, u32[]{:S(2)}, u32[]{:S(2)}) collective-permute-start(f32[6,2,4,64]{3,2,1,0:T(4,128)S(1)} %collective-permute-done.4), channel_id=1, source_target_pairs={{0,32},{32,64},{64,96},{96,128},{128,160},{160,192},{192,224},{224... | collective-permute-start | bytes 36872 | tf_op jit(solution)/shard_map/ppermute | solution.py:35
  42.5 3.4 %collective-permute-start.7 = (f32[6,2,4,64]{3,2,1,0:T(4,128)S(1)}, f32[6,2,4,64]{3,2,1,0:T(4,128)S(1)}, u32[]{:S(2)}, u32[]{:S(2)}) collective-permute-start(f32[6,2,4,64]{3,2,1,0:T(4,128)S(1)} %collective-permute-done.5), channel_id=1, source_target_pairs={{0,480},{32,0},{64,32},{96,64},{128,96},{160,128},{192,160},{224,1... | collective-permute-start | bytes 36872 | tf_op jit(solution)/shard_map/ppermute | solution.py:42
  45.7 4.5 %collective-permute-start.8 = (f32[6,2,4,64]{3,2,1,0:T(4,128)S(1)}, f32[6,2,4,64]{3,2,1,0:T(4,128)S(1)}, u32[]{:S(2)}, u32[]{:S(2)}) collective-permute-start(f32[6,2,4,64]{3,2,1,0:T(4,128)S(1)} %collective-permute-done.6), channel_id=1, source_target_pairs={{0,32},{32,64},{64,96},{96,128},{128,160},{160,192},{192,224},{224... | collective-permute-start | bytes 36872 | tf_op jit(solution)/shard_map/ppermute | solution.py:35
  45.9 4.5 %collective-permute-start.9 = (f32[6,2,4,64]{3,2,1,0:T(4,128)S(1)}, f32[6,2,4,64]{3,2,1,0:T(4,128)S(1)}, u32[]{:S(2)}, u32[]{:S(2)}) collective-permute-start(f32[6,2,4,64]{3,2,1,0:T(4,128)S(1)} %collective-permute-done.7), channel_id=1, source_target_pairs={{0,480},{32,0},{64,32},{96,64},{128,96},{160,128},{192,160},{224,1... | collective-permute-start | bytes 36872 | tf_op jit(solution)/shard_map/ppermute | solution.py:42
  50.2 4.5 %collective-permute-start.10 = (f32[6,2,4,64]{3,2,1,0:T(4,128)S(1)}, f32[6,2,4,64]{3,2,1,0:T(4,128)S(1)}, u32[]{:S(2)}, u32[]{:S(2)}) collective-permute-start(f32[6,2,4,64]{3,2,1,0:T(4,128)S(1)} %collective-permute-done.8), channel_id=1, source_target_pairs={{0,32},{32,64},{64,96},{96,128},{128,160},{160,192},{192,224},{224... | collective-permute-start | bytes 36872 | tf_op jit(solution)/shard_map/ppermute | solution.py:35
  50.3 4.5 %collective-permute-start.11 = (f32[6,2,4,64]{3,2,1,0:T(4,128)S(1)}, f32[6,2,4,64]{3,2,1,0:T(4,128)S(1)}, u32[]{:S(2)}, u32[]{:S(2)}) collective-permute-start(f32[6,2,4,64]{3,2,1,0:T(4,128)S(1)} %collective-permute-done.9), channel_id=1, source_target_pairs={{0,480},{32,0},{64,32},{96,64},{128,96},{160,128},{192,160},{224,1... | collective-permute-start | bytes 36872 | tf_op jit(solution)/shard_map/ppermute | solution.py:42
  54.6 4.5 %collective-permute-start.12 = (f32[6,2,4,64]{3,2,1,0:T(4,128)S(1)}, f32[6,2,4,64]{3,2,1,0:T(4,128)S(1)}, u32[]{:S(2)}, u32[]{:S(2)}) collective-permute-start(f32[6,2,4,64]{3,2,1,0:T(4,128)S(1)} %collective-permute-done.10), channel_id=1, source_target_pairs={{0,32},{32,64},{64,96},{96,128},{128,160},{160,192},{192,224},{224... | collective-permute-start | bytes 36872 | tf_op jit(solution)/shard_map/ppermute | solution.py:35
  54.8 4.5 %collective-permute-start.13 = (f32[6,2,4,64]{3,2,1,0:T(4,128)S(1)}, f32[6,2,4,64]{3,2,1,0:T(4,128)S(1)}, u32[]{:S(2)}, u32[]{:S(2)}) collective-permute-start(f32[6,2,4,64]{3,2,1,0:T(4,128)S(1)} %collective-permute-done.11), channel_id=1, source_target_pairs={{0,480},{32,0},{64,32},{96,64},{128,96},{160,128},{192,160},{224,1... | collective-permute-start | bytes 36872 | tf_op jit(solution)/shard_map/ppermute | solution.py:42
  59.1 4.5 %collective-permute-start.14 = (f32[6,2,4,64]{3,2,1,0:T(4,128)S(1)}, f32[6,2,4,64]{3,2,1,0:T(4,128)S(1)}, u32[]{:S(2)}, u32[]{:S(2)}) collective-permute-start(f32[6,2,4,64]{3,2,1,0:T(4,128)S(1)} %collective-permute-done.12), channel_id=1, source_target_pairs={{0,32},{32,64},{64,96},{96,128},{128,160},{160,192},{192,224},{224... | collective-permute-start | bytes 36872 | tf_op jit(solution)/shard_map/ppermute | solution.py:35
  63.7 30.4 %copy-start.5 = (bf16[6,2,64,64]{3,2,1,0:T(8,128)(2,1)}, bf16[6,2,64,64]{3,2,1,0:T(8,128)(2,1)S(1)}, u32[]{:S(2)}) copy-start(bf16[6,2,64,64]{3,2,1,0:T(8,128)(2,1)S(1)} %fusion.18) | copy-start | bytes 294916
  65.4 9.8 %copy-start.7 = (bf16[2048,128]{1,0:T(8,128)(2,1)S(1)}, bf16[2048,128]{1,0:T(8,128)(2,1)}, u32[]{:S(2)}) copy-start(bf16[2048,128]{1,0:T(8,128)(2,1)} %param.6) | copy-start | bytes 1572868
  65.4 22.6 %all-to-all-start = ((bf16[2048,64,2]{0,2,1:T(2,128)(2,1)}), bf16[2048,64,2]{0,2,1:T(2,128)(2,1)S(1)}, u32[]{:S(2)}, u32[]{:S(2)}) async-start(bf16[2048,64,2]{0,2,1:T(2,128)(2,1)} %copy.46), calls=%async_computation | async-start | bytes 1048576 | tf_op jit(solution)/shard_map/all_to_all | solution.py:96
  88.0 18.9 %all-to-all-start.2 = ((bf16[2048,64,2]{0,2,1:T(2,128)(2,1)}), bf16[2048,64,2]{0,2,1:T(2,128)(2,1)S(1)}, u32[]{:S(2)}, u32[]{:S(2)}) async-start(bf16[2048,64,2]{0,2,1:T(2,128)(2,1)} %copy.54), calls=%async_computation.2 | async-start | bytes 1048576 | tf_op jit(solution)/shard_map/all_to_all | solution.py:80
  106.9 18.7 %all-to-all-start.1 = ((bf16[2048,64,2]{0,2,1:T(2,128)(2,1)}), bf16[2048,64,2]{0,2,1:T(2,128)(2,1)S(1)}, u32[]{:S(2)}, u32[]{:S(2)}) async-start(bf16[2048,64,2]{0,2,1:T(2,128)(2,1)} %copy.50), calls=%async_computation.1 | async-start | bytes 1048576 | tf_op jit(solution)/shard_map/all_to_all | solution.py:81
  131.9 18.0 %all-to-all-start.5 = ((bf16[2048,64,2]{0,2,1:T(2,128)(2,1)}), bf16[2048,64,2]{0,2,1:T(2,128)(2,1)}, u32[]{:S(2)}, u32[]{:S(2)}) async-start(bf16[2048,64,2]{0,2,1:T(2,128)(2,1)} %copy.62), calls=%async_computation.5 | async-start | bytes 1048576 | tf_op jit(solution)/shard_map/all_to_all | solution.py:94
  149.9 17.6 %all-to-all-start.4 = ((bf16[2048,64,2]{0,2,1:T(2,128)(2,1)}), bf16[2048,64,2]{0,2,1:T(2,128)(2,1)}, u32[]{:S(2)}, u32[]{:S(2)}) async-start(bf16[2048,64,2]{0,2,1:T(2,128)(2,1)} %copy.59), calls=%async_computation.4 | async-start | bytes 1048576 | tf_op jit(solution)/shard_map/all_to_all | solution.py:108
  167.4 17.6 %all-to-all-start.3 = ((bf16[2048,64,2]{0,2,1:T(2,128)(2,1)}), bf16[2048,64,2]{0,2,1:T(2,128)(2,1)}, u32[]{:S(2)}, u32[]{:S(2)}) async-start(bf16[2048,64,2]{0,2,1:T(2,128)(2,1)} %copy.57), calls=%async_computation.3 | async-start | bytes 1048576 | tf_op jit(solution)/shard_map/all_to_all | solution.py:107
  172.0 158.4 %all-reduce.5.cloned.1.call-start = ((), (), s32[]{:S(2)}) async-start(), calls=%async_computation.6 | async-start | bytes 1572864
  192.1 1.4 copy-start.8
  192.1 1.4 copy-start
  196.9 133.6 %copy-start.12 = (f32[6,2,4,64]{3,2,1,0:T(4,128)S(1)}, f32[6,2,4,64]{3,2,1,0:T(4,128)}, u32[]{:S(2)}) copy-start(f32[6,2,4,64]{3,2,1,0:T(4,128)} %param.9) | copy-start | bytes 36868
  196.9 133.6 %copy-start.13 = (f32[6,2,4,64]{3,2,1,0:T(4,128)S(1)}, f32[6,2,4,64]{3,2,1,0:T(4,128)}, u32[]{:S(2)}) copy-start(f32[6,2,4,64]{3,2,1,0:T(4,128)} %param.10) | copy-start | bytes 36868
  196.9 133.6 %copy-start.10 = (f32[6,2,4,64]{3,2,1,0:T(4,128)S(1)}, f32[6,2,4,64]{3,2,1,0:T(4,128)}, u32[]{:S(2)}) copy-start(f32[6,2,4,64]{3,2,1,0:T(4,128)} %param.8) | copy-start | bytes 36868
  (4 other events, 3.9 us)
Sparse Core Ops, SparseCore 0:
  197.0 133.3 all-reduce.4
